TPU v7x, 32 devices: a whole 2x2x4 slice. The times are simulated.
32 devices in a mesh: row: 8 (over z, core), col: 4 (over y, x).
Axes of the slice: x: 2, y: 2, z: 4, core: 2. Of those that a mesh axis runs over, the one named last changes fastest.
Arguments:
- features: bfloat16 [9, 1, 128, 128, 128], P(None, None, 'row', 'col'), may hold values from -12 to 12
- cotangent: float32 [3, 1, 128, 128, 128], P(None, None, 'row', 'col'), may hold values from -14 to 14
- w_in: bfloat16 [9, 256], replicated, may hold values from -2 to 2
- bias_in: float32 [256], replicated, may hold values from -3 to 3
- w_mid: bfloat16 [256, 256], replicated, may hold values from -0.375 to 0.375
- bias_mid: float32 [256], replicated, may hold values from -3 to 3
- w_out: bfloat16 [256, 6], replicated, may hold values from -2.5 to 2.5
Outputs:
- grad_features: float32 [9, 1, 128, 128, 128], P(None, None, 'row', 'col')
- grad_w_in: float32 [9, 256], replicated
- grad_b_in: float32 [256], replicated
- grad_w_mid: float32 [256, 256], replicated
- grad_b_mid: float32 [256], replicated
- grad_w_out: float32 [256, 6], replicated
All inputs are finite; a program needn't handle non-finite values.
Results may differ from a plain program's by a relative error of at most 0.025.
Values sent between devices are 32-bit elements; how exact they have to be, the bound alone decides.
A program may use at most 128 MiB of HBM per device.

v0:
```python
import math
import jax
import jax.numpy as jnp
from jax import lax
from jax.sharding import PartitionSpec as P

NX = 128
NY = 128
NZ = 128
CELLS = 2097152
STEP_DT = 0.04
PAIRS = ((0, 0), (1, 1), (2, 2), (0, 1), (0, 2), (1, 2))


def mode_list(count, length):
    index = jnp.arange(count, dtype=jnp.int32)
    return jnp.where(index < length // 2, index, index - length)


def phase_table(modes, length):
    positions = jnp.arange(length, dtype=jnp.int32)
    turns = positions[:, None] * modes[None, :] % length
    angle = turns.astype(jnp.float32) * (2.0 * math.pi / length)
    return (jnp.cos(angle), jnp.sin(angle))


def contract(form, left, right):
    return jnp.einsum(
        form, left, right, precision=lax.Precision.HIGHEST, preferred_element_type=jnp.float32
    )


def complex_product(form, part, table_real, table_imag):
    real = contract(form, part[0], table_real) - contract(form, part[1], table_imag)
    imag = contract(form, part[0], table_imag) + contract(form, part[1], table_real)
    return jnp.stack([real, imag])


def closure_block(x_blk, g_blk, w_in, bias_in, w_mid, bias_mid, w_out):
    pre_in = (
        jnp.einsum("fh,fn->hn", w_in, x_blk, preferred_element_type=jnp.float32) + bias_in[:, None]
    )
    act_in = jnp.tanh(pre_in).astype(jnp.bfloat16)
    pre_mid = (
        jnp.einsum("io,in->on", w_mid, act_in, preferred_element_type=jnp.float32)
        + bias_mid[:, None]
    )
    act_mid = jnp.tanh(pre_mid).astype(jnp.bfloat16)
    back_mid = jnp.einsum("ho,on->hn", w_out, g_blk, preferred_element_type=jnp.float32)
    delta_mid = (back_mid * (1.0 - jnp.square(act_mid.astype(jnp.float32)))).astype(jnp.bfloat16)
    back_in = jnp.einsum("io,on->in", w_mid, delta_mid, preferred_element_type=jnp.float32)
    delta_in = (back_in * (1.0 - jnp.square(act_in.astype(jnp.float32)))).astype(jnp.bfloat16)
    grad_x = jnp.einsum("fh,hn->fn", w_in, delta_in, preferred_element_type=jnp.float32)
    gw_out = jnp.einsum("hn,on->ho", act_mid, g_blk, preferred_element_type=jnp.float32)
    gw_mid = jnp.einsum("in,on->io", act_in, delta_mid, preferred_element_type=jnp.float32)
    gw_in = jnp.einsum("fn,hn->fh", x_blk, delta_in, preferred_element_type=jnp.float32)
    gb_mid = jnp.sum(delta_mid.astype(jnp.float32), axis=1)
    gb_in = jnp.sum(delta_in.astype(jnp.float32), axis=1)
    return (grad_x, (gw_in, gb_in, gw_mid, gb_mid, gw_out))


def per_device(features, cotangent, w_in, bias_in, w_mid, bias_mid, w_out):
    rows_group = lax.axis_size("row")
    cols_group = lax.axis_size("col")
    count_y = NY
    count_z = NZ
    list_z = mode_list(count_z, NZ)
    weight_z = jnp.ones((count_z,), jnp.float32) / NZ
    list_x = mode_list(NX, NX)
    list_y = mode_list(count_y, NY)
    cos_x, sin_x = phase_table(list_x, NX)
    cos_y, sin_y = phase_table(list_y, NY)
    cos_z, sin_z = phase_table(list_z, NZ)
    forward_z = jnp.stack(
        [
            contract("csxyz,zk->csxky", cotangent, cos_z),
            -contract("csxyz,zk->csxky", cotangent, sin_z),
        ]
    )
    spectra = complex_product(
        "csxky,yq->cskqx",
        lax.all_to_all(forward_z, "col", split_axis=4, concat_axis=5, tiled=True),
        cos_y,
        -sin_y,
    )
    spectra = complex_product(
        "cskqx,xp->cskqp",
        lax.all_to_all(spectra, "row", split_axis=4, concat_axis=5, tiled=True),
        cos_x,
        -sin_x,
    )
    share_y = count_y // rows_group
    share_z = count_z // cols_group
    local_y = lax.dynamic_slice_in_dim(list_y, lax.axis_index("row") * share_y, share_y)
    local_z = lax.dynamic_slice_in_dim(list_z, lax.axis_index("col") * share_z, share_z)
    modes_x = list_x[None, None, :]
    modes_y = local_y[None, :, None]
    modes_z = local_z[:, None, None]
    keep = (3 * jnp.abs(modes_x) < NX) & (3 * jnp.abs(modes_y) < NY) & (3 * jnp.abs(modes_z) < NZ)
    waves = [modes_x.astype(jnp.float32), modes_y.astype(jnp.float32), modes_z.astype(jnp.float32)]
    velocity = [spectra[:, comp] for comp in range(3)]
    inner = waves[0] * velocity[0] + waves[1] * velocity[1] + waves[2] * velocity[2]
    square = jnp.maximum(waves[0] * waves[0] + waves[1] * waves[1] + waves[2] * waves[2], 1.0)
    projected = [
        jnp.where(keep, velocity[comp] - waves[comp] * inner / square, 0.0) for comp in range(3)
    ]
    stress_parts = []
    for first, second in PAIRS:
        if first == second:
            value = waves[first] * projected[first]
        else:
            value = waves[second] * projected[first] + waves[first] * projected[second]
        stress_parts.append(jnp.stack([-STEP_DT * value[1], STEP_DT * value[0]]))
    stress_hat = jnp.stack(stress_parts, axis=1)
    back_x = complex_product("cskqp,px->cskxq", stress_hat, cos_x.T / NX, sin_x.T / NX)
    stress_mid = complex_product(
        "cskxq,qy->csxyk",
        lax.all_to_all(back_x, "row", split_axis=4, concat_axis=5, tiled=True),
        cos_y.T / NY,
        sin_y.T / NY,
    )
    real_z = cos_z.T * weight_z[:, None]
    imag_z = sin_z.T * weight_z[:, None]
    part = lax.all_to_all(stress_mid, "col", split_axis=4, concat_axis=5, tiled=True)
    stress = contract("csxyk,kz->csxyz", part[0], real_z) - contract(
        "csxyk,kz->csxyz", part[1], imag_z
    )
    inputs_count = features.shape[0]
    stress_count = stress.shape[0]
    cells = stress.shape[1] * stress.shape[2] * stress.shape[3] * stress.shape[4]
    feats = features.reshape(inputs_count, cells)
    grads = stress.astype(jnp.bfloat16).reshape(stress_count, cells)
    hidden = w_mid.shape[0]
    blank = jnp.zeros((inputs_count, cells), jnp.float32)
    block = math.gcd(cells, max(1024, cells // 8))

    def visit(index, carry):
        current, totals = carry
        start = (0 + index * block).astype(jnp.int32)
        x_blk = lax.dynamic_slice_in_dim(feats, start, block, 1)
        g_blk = lax.dynamic_slice_in_dim(grads, start, block, 1)
        grad_x, parts = closure_block(x_blk, g_blk, w_in, bias_in, w_mid, bias_mid, w_out)
        current = lax.dynamic_update_slice_in_dim(current, grad_x, start, 1)
        return (current, tuple((a + b for a, b in zip(totals, parts))))

    init = (
        jnp.zeros((inputs_count, hidden), jnp.float32),
        jnp.zeros((hidden,), jnp.float32),
        jnp.zeros((hidden, hidden), jnp.float32),
        jnp.zeros((hidden,), jnp.float32),
        jnp.zeros((hidden, stress_count), jnp.float32),
    )
    field, local = lax.fori_loop(0, cells // block, visit, (blank, init))
    totals = lax.psum((local[0], local[1], local[2], local[3], local[4]), ("row", "col"))
    factor = 1.0 / math.sqrt(CELLS)
    return (
        field.reshape(features.shape),
        totals[0] * factor,
        totals[1] * factor,
        totals[2] * factor,
        totals[3] * factor,
        totals[4] * factor,
    )


def solution(mesh):
    return jax.shard_map(
        per_device,
        mesh=mesh,
        in_specs=(
            P(None, None, "row", "col", None),
            P(None, None, "row", "col", None),
            P(),
            P(),
            P(),
            P(),
            P(),
        ),
        out_specs=(P(None, None, "row", "col", None), P(), P(), P(), P(), P()),
        check_vma=False,
    )
```

profile of v0, /device:TPU:0, one launch (start us, length us, event | category | flops | bytes accessed | tf_op | source)
XLA Modules:
  0.0 856.4 jit_solution(18035341283685795229)
XLA Ops:
  22.5 25.4 %all_to_all.60 = f32[4,1,98304]{2,1,0:T(1,128)S(1)} all-to-all(f32[4,1,98304]{2,1,0:T(1,128)} %reshape.562), channel_id=1, replica_groups=mesh['row'=8,'col'=4] {'col'}, dimensions={0} | all-to-all | bytes 3145728 | tf_op jit(solution)/shard_map/all_to_all | solution.py:82
  87.1 7.6 reshape.564
  100.6 36.9 %all-to-all-done.1 = f32[8,1,49152]{2,1,0:T(1,128)S(1)} async-done(((f32[8,1,49152]{2,1,0:T(1,128)}), f32[8,1,49152]{2,1,0:T(1,128)S(1)}, u32[]{:S(2)}, u32[]{:S(2)}) %all-to-all-start.1) | async-done | bytes 1572896 | tf_op jit(solution)/shard_map/all_to_all | solution.py:88
  186.4 11.4 %copy.63 = f32[2,6,1,32,128,16]{3,5,1,2,0,4:T(8,128)} copy(f32[2,6,1,32,128,16]{4,3,5,1,2,0:T(8,128)} %pad_maximum_fusion) | data formatting | bytes 6291456 | tf_op jit(solution)/shard_map/stack | solution.py:36
  197.8 10.6 %reshape.566 = f32[8,1,98304]{2,1,0:T(1,128)} reshape(f32[128,2,1,6,16,32]{5,4,3,2,1,0:T(8,128)} %bitcast.283) | data formatting | bytes 6291456
  208.5 76.0 %all_to_all.61 = f32[8,1,98304]{2,1,0:T(1,128)} all-to-all(f32[8,1,98304]{2,1,0:T(1,128)} %reshape.566), channel_id=1, replica_groups=mesh['row'=8,'col'=4] {'row'}, dimensions={0} | all-to-all | bytes 6291456 | tf_op jit(solution)/shard_map/all_to_all | solution.py:118
  284.4 11.7 %reduce.4 = f32[8,98304]{1,0:T(8,128)} reduce(f32[8,1,98304]{2,1,0:T(1,128)} %all_to_all.61, f32[]{:T(128)} %broadcast.808), dimensions={1}, to_apply=%all_to_all.50.reduce_sub_computation | reduce | bytes 6291460 | tf_op jit(solution)/shard_map/all_to_all | solution.py:118
  296.1 10.9 %reshape.567 = f32[128,2,1,6,16,32]{5,4,3,2,1,0:T(8,128)} reshape(f32[8,98304]{1,0:T(8,128)} %reduce.4) | data formatting | bytes 6291456
  307.0 10.4 %copy.64 = f32[2,6,1,32,128,16]{3,5,4,1,0,2:T(8,128)} copy(f32[2,6,1,32,128,16]{3,5,1,2,0,4:T(8,128)} %bitcast.281) | data formatting | bytes 6291456 | tf_op jit(solution)/shard_map/all_to_all | solution.py:118
  317.4 10.7 %fusion.205 = (f32[1,6,1,32,16,8,16]{3,6,4,5,1,0,2:T(8,128)}, f32[1,6,1,32,16,8,16]{3,6,4,5,1,0,2:T(8,128)}) fusion(f32[2,6,1,32,16,8,16]{3,6,4,5,1,0,2:T(8,128)} %bitcast.279), kind=kLoop, calls=%fused_computation.273 | loop fusion | bytes 6291456 | tf_op jit(solution)/shard_map/slice | solution.py:34
  331.8 10.1 %fusion.64 = f32[128,6,32,16]{0,2,3,1:T(8,128)S(1)} fusion(f32[6,32,16,128]{1,3,2,0:T(8,128)S(1)} %bitcast.277, s32[128]{0:T(128)S(1)} %compare_select_fusion), kind=kOutput, calls=%fused_computation.138 | convolution fusion | flops 604225536 | bytes 3146240 | tf_op jit(solution)/shard_map/cskxq,qy->csxyk/dot_general | solution.py:28
  341.9 10.2 %fusion.43 = f32[128,6,32,16]{0,2,3,1:T(8,128)S(1)} fusion(f32[6,32,16,128]{1,3,2,0:T(8,128)S(1)} %bitcast.278, s32[128]{0:T(128)S(1)} %compare_select_fusion), kind=kOutput, calls=%fused_computation.117 | convolution fusion | flops 604225536 | bytes 3146240 | tf_op jit(solution)/shard_map/cskxq,qy->csxyk/dot_general | solution.py:28
  353.1 10.5 %subtract_bitcast_fusion = f32[1,6,1,16,128,32]{4,5,3,1,2,0:T(8,128)S(1)} fusion(f32[128,6,32,16]{0,2,3,1:T(8,128)S(1)} %fusion.64, f32[6,32,16,128]{1,3,2,0:T(8,128)S(1)} %bitcast.275, s32[128]{0:T(128)S(1)} %compare_select_fusion), kind=kOutput, calls=%fused_computation.41 | convolution fusion | flops 604618752 | bytes 4719104 | tf_op jit(solution)/shard_map/cskxq,qy->csxyk/dot_general | solution.py:28
  363.6 10.1 %add_bitcast_fusion = f32[1,6,1,16,128,32]{4,5,3,1,2,0:T(8,128)S(1)} fusion(f32[128,6,32,16]{0,2,3,1:T(8,128)S(1)} %fusion.43, f32[6,32,16,128]{1,3,2,0:T(8,128)S(1)} %bitcast.276, s32[128]{0:T(128)S(1)} %compare_select_fusion), kind=kOutput, calls=%fused_computation.40 | convolution fusion | flops 604618752 | bytes 4719104 | tf_op jit(solution)/shard_map/cskxq,qy->csxyk/dot_general | solution.py:28
  375.7 11.4 %copy.71 = f32[2,6,1,16,128,32]{5,3,1,2,0,4:T(8,128)} copy(f32[2,6,1,16,128,32]{4,5,3,1,2,0:T(8,128)} %pad_maximum_fusion.1) | data formatting | bytes 6291456 | tf_op jit(solution)/shard_map/stack | solution.py:36
  387.1 9.3 %reshape.568 = f32[4,1,196608]{2,1,0:T(1,128)} reshape(f32[128,2,1,6,16,32]{5,4,3,2,1,0:T(8,128)} %bitcast.284) | data formatting | bytes 6291456
  404.2 33.1 %all-to-all-done.3 = f32[4,1,196608]{2,1,0:T(1,128)} async-done(((f32[4,1,196608]{2,1,0:T(1,128)}), f32[4,1,196608]{2,1,0:T(1,128)}, u32[]{:S(2)}, u32[]{:S(2)}) %all-to-all-start.3) | async-done | bytes 3145760 | tf_op jit(solution)/shard_map/all_to_all | solution.py:124
  437.3 11.8 %reduce.5 = f32[4,196608]{1,0:T(4,128)} reduce(f32[4,1,196608]{2,1,0:T(1,128)} %all-to-all-done.3, f32[]{:T(128)} %broadcast.808), dimensions={1}, to_apply=%all_to_all.53.reduce_sub_computation | reduce | bytes 6291460 | tf_op jit(solution)/shard_map/all_to_all | solution.py:124
  449.1 10.7 %reshape.569 = f32[128,2,1,6,16,32]{5,4,3,2,1,0:T(8,128)} reshape(f32[4,196608]{1,0:T(4,128)} %reduce.5) | data formatting | bytes 6291456
  459.9 16.4 %copy.94 = f32[2,6,1,16,4,32,32]{6,4,5,3,1,2,0:T(4,128)} copy(f32[2,6,1,16,4,32,32]{6,3,1,0,5,4,2:T(8,128)} %bitcast.282) | data formatting | bytes 6291456 | tf_op jit(solution)/shard_map/all_to_all | solution.py:124
  476.3 14.3 %fusion.204 = (f32[1,6,1,16,32,4,32]{6,5,4,3,1,2,0:T(4,128)}, f32[1,6,1,16,32,4,32]{6,5,4,3,1,2,0:T(4,128)}) fusion(f32[2,6,1,16,32,4,32]{6,5,4,3,1,2,0:T(4,128)} %bitcast.280), kind=kLoop, calls=%fused_computation.272 | loop fusion | bytes 6291456 | tf_op jit(solution)/shard_map/slice | solution.py:126
  511.5 165.8 %while.24 = (s32[]{:T(128)}, f32[9,65536]{1,0:T(8,128)}, f32[9,256]{1,0:T(8,128)S(1)}, f32[256]{0:T(256)S(1)}, f32[256,256]{1,0:T(8,128)S(1)}, /*index=5*/f32[25...) while((s32[]{:T(128)}, f32[9,65536]{1,0:T(8,128)}, ...), condition=%wide.region_3.4_spmd.clone, body=%wide.region_0.3_spmd.clone.sunk | while | flops 3422691328 | bytes 157343136 | solution.py:153
  677.3 37.5 %all-reduce = (f32[9,256]{1,0:T(8,128)S(1)}, f32[256]{0:T(256)S(1)}, f32[256]{0:T(256)S(1)}, f32[256,6]{0,1:T(8,128)S(1)}) all-reduce(f32[9,256]{1,0:T(8,128)S(1)} %get-tuple-element.241, f32[256]{0:T(256)S(1)} %get-tuple-element.242, f32[256]{0:T(256)S(1)} %get-tuple-element.244, ...), channel_id=1, replica_groups=mesh['row'=8,'col'=4] {'row','col'}, use_global_device_ids=true, to_apply=%region_4.5 | all-reduce | flops 4352 | bytes 34816 | tf_op jit(solution)/shard_map/psum | solution.py:154
  721.8 125.8 %all-reduce.3.cloned.1.call-done = f32[256,256]{1,0:T(8,128)} async-done(((f32[256,256]{1,0:T(8,128)}), f32[256,256]{1,0:T(8,128)}) %all-reduce.3.cloned.1.call-update) | async-done | bytes 262160 | tf_op jit(solution)/shard_map/psum | solution.py:154
  (276 shorter events, 317.6 us)
Async XLA Ops:
  94.7 42.8 %all-to-all-start.1 = ((f32[8,1,49152]{2,1,0:T(1,128)}), f32[8,1,49152]{2,1,0:T(1,128)S(1)}, u32[]{:S(2)}, u32[]{:S(2)}) async-start(f32[8,1,49152]{2,1,0:T(1,128)} %reshape.564), calls=%async_computation.1 | async-start | bytes 3145728 | tf_op jit(solution)/shard_map/all_to_all | solution.py:88
  331.8 20.3 %slice-start = ((s8[6291456]{0:T(1024)(128)(4,1)}), s8[4194304]{0:T(1024)(128)(4,1)S(1)}, s32[]{:S(2)}) async-start(s8[6291456]{0:T(1024)(128)(4,1)} %bitcast.291), calls=%async_computation.5 | async-start | bytes 8388608
  341.9 10.3 %slice-start.1 = ((s8[6291456]{0:T(1024)(128)(4,1)}), s8[2097152]{0:T(1024)(128)(4,1)S(1)}, s32[]{:S(2)}) async-start(s8[6291456]{0:T(1024)(128)(4,1)} %bitcast.291), calls=%async_computation.6 | async-start | bytes 4194304
  396.4 4.9 copy-start.9
  396.4 40.9 %all-to-all-start.3 = ((f32[4,1,196608]{2,1,0:T(1,128)}), f32[4,1,196608]{2,1,0:T(1,128)}, u32[]{:S(2)}, u32[]{:S(2)}) async-start(f32[4,1,196608]{2,1,0:T(1,128)} %reshape.568), calls=%async_computation.3 | async-start | bytes 6291456 | tf_op jit(solution)/shard_map/all_to_all | solution.py:124
  401.2 446.4 %all-reduce.3.cloned.1.call-start = ((), (), s32[]{:S(2)}) async-start(), calls=%async_computation.4 | async-start | bytes 524288 | tf_op jit(solution)/shard_map/psum | solution.py:154
  517.5 4.0 copy-start.5
  521.4 4.4 copy-start.4
  538.2 4.0 copy-start.5
  542.1 4.4 copy-start.4
  558.8 4.0 copy-start.5
  562.8 4.4 copy-start.4
  579.5 4.0 copy-start.5
  583.5 4.4 copy-start.4
  600.2 4.0 copy-start.5
  604.2 4.4 copy-start.4
  620.9 4.0 copy-start.5
  624.9 4.4 copy-start.4
  641.6 4.0 copy-start.5
  645.6 4.4 copy-start.4
  662.3 4.0 copy-start.5
  666.3 4.3 copy-start.4
  677.3 42.4 %copy-start.8 = (f32[256,256]{1,0:T(8,128)}, f32[256,256]{1,0:T(8,128)S(1)}, u32[]{:S(2)}) copy-start(f32[256,256]{1,0:T(8,128)S(1)} %get-tuple-element.243) | copy-start | bytes 786436
  716.5 132.8 %copy-start.1 = (f32[3,1,16,32,128]{4,3,2,1,0:T(8,128)S(1)}, f32[3,1,16,32,128]{4,3,2,1,0:T(8,128)}, u32[]{:S(2)}) copy-start(f32[3,1,16,32,128]{4,3,2,1,0:T(8,128)} %param.10) | copy-start | bytes 2359300
  (38 other events, 106.6 us)
Sparse Core Ops, SparseCore 0:
  721.3 126.2 all-reduce.2
where the time goes:
time: 862 us; the launch traced here: 856 us
  matrix products  242 us (28%)
  local copies, waits for them, and re-layouts  207 us (24%)
  waiting for transfers between devices  196 us (23%)
  blocking collectives  139 us (16%)
  other arithmetic  46.9 us (5%)
  between operations  14.9 us (2%)
  starting transfers between devices  9.97 us (1%)
    psum x1, waiting for transfers between devices, per_device(): lax.psum((local[0], local[1], local[2], local[3], local[4]), ('row', 'col'))  126 us
    dot_general x20, matrix products, contract(): jnp.einsum(form, left, right, precision=lax.Precision.HIGHEST, preferred_...  81.1 us
    unnamed x35, local copies, waits for them, and re-layouts  76.7 us
    all_to_all x1, blocking collectives, per_device(): lax.all_to_all(back_x, 'row', split_axis=4, concat_axis=5, tiled=True)  76 us
    psum x1, blocking collectives, per_device(): lax.psum((local[0], local[1], local[2], local[3], local[4]), ('row', 'col'))  37.5 us
    all_to_all x1, waiting for transfers between devices, per_device(): lax.all_to_all(spectra, 'row', split_axis=4, concat_axis=5, tiled=True)  36.9 us
    dot_general x8, matrix products, closure_block(): jnp.einsum('fh,hn->fn', w_in, delta_in, preferred_element_type=jnp.float32)  34.8 us
    all_to_all x1, waiting for transfers between devices, per_device(): lax.all_to_all(stress_mid, 'col', split_axis=4, concat_axis=5, tiled=True)  33.1 us
  transfers between devices with their start and end apart: 3, of which 3 were waited for; matrix products, arithmetic and copies ran while one was open for 0% of the time, Pallas kernels for 0%

commit v1 on v0

--- a/solution.py
+++ b/solution.py
@@ -151,7 +151,7 @@
         jnp.zeros((hidden, stress_count), jnp.float32),
     )
     field, local = lax.fori_loop(0, cells // block, visit, (blank, init))
-    totals = lax.psum((local[0], local[1], local[2], local[3], local[4]), ("row", "col"))
+    totals = lax.psum(lax.psum((local[0], local[1], local[2], local[3], local[4]), "col"), "row")
     factor = 1.0 / math.sqrt(CELLS)
     return (
         field.reshape(features.shape),

time: 862 us -> 831 us (0.964)
  waiting for transfers between devices: 196 us -> 161 us
    psum x1 -> x2, waiting for transfers between devices: 126 us -> 91.1 us  [the longest x1 56.7 us: per_device(): lax.psum(lax.psum((local[0], local[1], local[2], local[3], local[4]), 'co...]
    psum x1 -> x2, blocking collectives: 37.5 us -> 41.3 us  [the longest x1 26 us: per_device(): lax.psum(lax.psum((local[0], local[1], local[2], local[3], local[4]), 'co...]
  transfers between devices with their start and end apart: 3 -> 4, of which waited for: 3 -> 4; matrix products, arithmetic and copies ran while one was open for 0% -> 1% of each run, Pallas kernels for 0% -> 0%
where the time goes in v1:
time: 831 us; the launch traced here: 826 us
  matrix products  242 us (29%)
  local copies, waits for them, and re-layouts  208 us (25%)
  waiting for transfers between devices  161 us (19%)
  blocking collectives  143 us (17%)
  other arithmetic  46.9 us (6%)
  between operations  14.9 us (2%)
  starting transfers between devices  10 us (1%)
    dot_general x20, matrix products, contract(): jnp.einsum(form, left, right, precision=lax.Precision.HIGHEST, preferred_...  81.1 us
    unnamed x35, local copies, waits for them, and re-layouts  76.8 us
    all_to_all x1, blocking collectives, per_device(): lax.all_to_all(back_x, 'row', split_axis=4, concat_axis=5, tiled=True)  76 us
    psum x1, waiting for transfers between devices, per_device(): lax.psum(lax.psum((local[0], local[1], local[2], local[3], local[4]), 'co...  56.7 us
    all_to_all x1, waiting for transfers between devices, per_device(): lax.all_to_all(spectra, 'row', split_axis=4, concat_axis=5, tiled=True)  36.9 us
    dot_general x8, matrix products, closure_block(): jnp.einsum('fh,hn->fn', w_in, delta_in, preferred_element_type=jnp.float32)  34.8 us
    psum x1, waiting for transfers between devices, per_device(): lax.psum((local[0], local[1], local[2], local[3], local[4]), 'col')  34.3 us
    all_to_all x1, waiting for transfers between devices, per_device(): lax.all_to_all(stress_mid, 'col', split_axis=4, concat_axis=5, tiled=True)  33.1 us
  transfers between devices with their start and end apart: 4, of which 4 were waited for; matrix products, arithmetic and copies ran while one was open for 1% of the time, Pallas kernels for 0%

profile of v1, /device:TPU:0, one launch (start us, length us, event | category | flops | bytes accessed | tf_op | source)
XLA Modules:
  0.0 825.8 jit_solution(17693745026779628613)
XLA Ops:
  22.6 25.4 %all_to_all.60 = f32[4,1,98304]{2,1,0:T(1,128)S(1)} all-to-all(f32[4,1,98304]{2,1,0:T(1,128)} %reshape.562), channel_id=1, replica_groups=mesh['row'=8,'col'=4] {'col'}, dimensions={0} | all-to-all | bytes 3145728 | tf_op jit(solution)/shard_map/all_to_all | solution.py:82
  100.8 36.9 %all-to-all-done.1 = f32[8,1,49152]{2,1,0:T(1,128)S(1)} async-done(((f32[8,1,49152]{2,1,0:T(1,128)}), f32[8,1,49152]{2,1,0:T(1,128)S(1)}, u32[]{:S(2)}, u32[]{:S(2)}) %all-to-all-start.1) | async-done | bytes 1572896 | tf_op jit(solution)/shard_map/all_to_all | solution.py:88
  186.6 11.4 %copy.63 = f32[2,6,1,32,128,16]{3,5,1,2,0,4:T(8,128)} copy(f32[2,6,1,32,128,16]{4,3,5,1,2,0:T(8,128)} %pad_maximum_fusion) | data formatting | bytes 6291456 | tf_op jit(solution)/shard_map/stack | solution.py:36
  198.1 10.7 %reshape.566 = f32[8,1,98304]{2,1,0:T(1,128)} reshape(f32[128,2,1,6,16,32]{5,4,3,2,1,0:T(8,128)} %bitcast.283) | data formatting | bytes 6291456
  208.7 76.0 %all_to_all.61 = f32[8,1,98304]{2,1,0:T(1,128)} all-to-all(f32[8,1,98304]{2,1,0:T(1,128)} %reshape.566), channel_id=1, replica_groups=mesh['row'=8,'col'=4] {'row'}, dimensions={0} | all-to-all | bytes 6291456 | tf_op jit(solution)/shard_map/all_to_all | solution.py:118
  284.7 11.7 %reduce.4 = f32[8,98304]{1,0:T(8,128)} reduce(f32[8,1,98304]{2,1,0:T(1,128)} %all_to_all.61, f32[]{:T(128)} %broadcast.808), dimensions={1}, to_apply=%all_to_all.50.reduce_sub_computation | reduce | bytes 6291460 | tf_op jit(solution)/shard_map/all_to_all | solution.py:118
  296.4 10.9 %reshape.567 = f32[128,2,1,6,16,32]{5,4,3,2,1,0:T(8,128)} reshape(f32[8,98304]{1,0:T(8,128)} %reduce.4) | data formatting | bytes 6291456
  307.3 10.4 %copy.64 = f32[2,6,1,32,128,16]{3,5,4,1,0,2:T(8,128)} copy(f32[2,6,1,32,128,16]{3,5,1,2,0,4:T(8,128)} %bitcast.281) | data formatting | bytes 6291456 | tf_op jit(solution)/shard_map/all_to_all | solution.py:118
  317.6 10.7 %fusion.205 = (f32[1,6,1,32,16,8,16]{3,6,4,5,1,0,2:T(8,128)}, f32[1,6,1,32,16,8,16]{3,6,4,5,1,0,2:T(8,128)}) fusion(f32[2,6,1,32,16,8,16]{3,6,4,5,1,0,2:T(8,128)} %bitcast.279), kind=kLoop, calls=%fused_computation.273 | loop fusion | bytes 6291456 | tf_op jit(solution)/shard_map/slice | solution.py:34
  332.1 10.1 %fusion.64 = f32[128,6,32,16]{0,2,3,1:T(8,128)S(1)} fusion(f32[6,32,16,128]{1,3,2,0:T(8,128)S(1)} %bitcast.277, s32[128]{0:T(128)S(1)} %compare_select_fusion), kind=kOutput, calls=%fused_computation.138 | convolution fusion | flops 604225536 | bytes 3146240 | tf_op jit(solution)/shard_map/cskxq,qy->csxyk/dot_general | solution.py:28
  342.2 10.2 %fusion.43 = f32[128,6,32,16]{0,2,3,1:T(8,128)S(1)} fusion(f32[6,32,16,128]{1,3,2,0:T(8,128)S(1)} %bitcast.278, s32[128]{0:T(128)S(1)} %compare_select_fusion), kind=kOutput, calls=%fused_computation.117 | convolution fusion | flops 604225536 | bytes 3146240 | tf_op jit(solution)/shard_map/cskxq,qy->csxyk/dot_general | solution.py:28
  353.4 10.5 %subtract_bitcast_fusion = f32[1,6,1,16,128,32]{4,5,3,1,2,0:T(8,128)S(1)} fusion(f32[128,6,32,16]{0,2,3,1:T(8,128)S(1)} %fusion.64, f32[6,32,16,128]{1,3,2,0:T(8,128)S(1)} %bitcast.275, s32[128]{0:T(128)S(1)} %compare_select_fusion), kind=kOutput, calls=%fused_computation.41 | convolution fusion | flops 604618752 | bytes 4719104 | tf_op jit(solution)/shard_map/cskxq,qy->csxyk/dot_general | solution.py:28
  363.9 10.1 %add_bitcast_fusion = f32[1,6,1,16,128,32]{4,5,3,1,2,0:T(8,128)S(1)} fusion(f32[128,6,32,16]{0,2,3,1:T(8,128)S(1)} %fusion.43, f32[6,32,16,128]{1,3,2,0:T(8,128)S(1)} %bitcast.276, s32[128]{0:T(128)S(1)} %compare_select_fusion), kind=kOutput, calls=%fused_computation.40 | convolution fusion | flops 604618752 | bytes 4719104 | tf_op jit(solution)/shard_map/cskxq,qy->csxyk/dot_general | solution.py:28
  376.0 11.4 %copy.71 = f32[2,6,1,16,128,32]{5,3,1,2,0,4:T(8,128)} copy(f32[2,6,1,16,128,32]{4,5,3,1,2,0:T(8,128)} %pad_maximum_fusion.1) | data formatting | bytes 6291456 | tf_op jit(solution)/shard_map/stack | solution.py:36
  404.5 33.1 %all-to-all-done.3 = f32[4,1,196608]{2,1,0:T(1,128)} async-done(((f32[4,1,196608]{2,1,0:T(1,128)}), f32[4,1,196608]{2,1,0:T(1,128)}, u32[]{:S(2)}, u32[]{:S(2)}) %all-to-all-start.3) | async-done | bytes 3145760 | tf_op jit(solution)/shard_map/all_to_all | solution.py:124
  437.6 11.8 %reduce.5 = f32[4,196608]{1,0:T(4,128)} reduce(f32[4,1,196608]{2,1,0:T(1,128)} %all-to-all-done.3, f32[]{:T(128)} %broadcast.808), dimensions={1}, to_apply=%all_to_all.53.reduce_sub_computation | reduce | bytes 6291460 | tf_op jit(solution)/shard_map/all_to_all | solution.py:124
  449.4 10.7 %reshape.569 = f32[128,2,1,6,16,32]{5,4,3,2,1,0:T(8,128)} reshape(f32[4,196608]{1,0:T(4,128)} %reduce.5) | data formatting | bytes 6291456
  460.2 16.4 %copy.94 = f32[2,6,1,16,4,32,32]{6,4,5,3,1,2,0:T(4,128)} copy(f32[2,6,1,16,4,32,32]{6,3,1,0,5,4,2:T(8,128)} %bitcast.282) | data formatting | bytes 6291456 | tf_op jit(solution)/shard_map/all_to_all | solution.py:124
  476.6 14.3 %fusion.204 = (f32[1,6,1,16,32,4,32]{6,5,4,3,1,2,0:T(4,128)}, f32[1,6,1,16,32,4,32]{6,5,4,3,1,2,0:T(4,128)}) fusion(f32[2,6,1,16,32,4,32]{6,5,4,3,1,2,0:T(4,128)} %bitcast.280), kind=kLoop, calls=%fused_computation.272 | loop fusion | bytes 6291456 | tf_op jit(solution)/shard_map/slice | solution.py:126
  511.8 165.7 %while.24 = (s32[]{:T(128)}, f32[9,65536]{1,0:T(8,128)}, f32[9,256]{1,0:T(8,128)S(1)}, f32[256]{0:T(256)S(1)}, f32[256,256]{1,0:T(8,128)S(1)}, /*index=5*/f32[25...) while((s32[]{:T(128)}, f32[9,65536]{1,0:T(8,128)}, ...), condition=%wide.region_3.4_spmd.clone, body=%wide.region_0.3_spmd.clone.sunk | while | flops 3422691328 | bytes 157343136 | solution.py:153
  677.4 15.3 %all-reduce.1 = (f32[9,256]{1,0:T(8,128)S(1)}, f32[256]{0:T(256)S(1)}, f32[256]{0:T(256)S(1)}, f32[256,6]{0,1:T(8,128)S(1)}) all-reduce(f32[9,256]{1,0:T(8,128)S(1)} %get-tuple-element.241, f32[256]{0:T(256)S(1)} %get-tuple-element.242, f32[256]{0:T(256)S(1)} %get-tuple-element.244, ...), channel_id=1, replica_groups=mesh['row'=8,'col'=4] {'col'}, use_global_device_ids=true, to_apply=%region_4.5 | all-reduce | flops 4352 | bytes 34816 | tf_op jit(solution)/shard_map/psum | solution.py:154
  692.8 26.0 %all-reduce = (f32[9,256]{1,0:T(8,128)S(1)}, f32[256]{0:T(256)S(1)}, f32[256]{0:T(256)S(1)}, f32[256,6]{0,1:T(8,128)S(1)}) all-reduce(f32[9,256]{1,0:T(8,128)S(1)} %get-tuple-element.323, f32[256]{0:T(256)S(1)} %get-tuple-element.324, f32[256]{0:T(256)S(1)} %get-tuple-element.325, ...), channel_id=1, replica_groups=mesh['row'=8,'col'=4] {'row'}, use_global_device_ids=true, to_apply=%region_5.6 | all-reduce | flops 4352 | bytes 34816 | tf_op jit(solution)/shard_map/psum | solution.py:154
  725.3 34.3 %all-reduce.5.cloned.1.call-done = f32[256,256]{1,0:T(8,128)} async-done(((f32[256,256]{1,0:T(8,128)}), f32[256,256]{1,0:T(8,128)}) %all-reduce.5.cloned.1.call-update) | async-done | bytes 262160 | tf_op jit(solution)/shard_map/psum | solution.py:154
  760.2 56.7 %all-reduce.7.cloned.1.call-done = f32[256,256]{1,0:T(8,128)} async-done(((f32[256,256]{1,0:T(8,128)}), f32[256,256]{1,0:T(8,128)}) %all-reduce.7.cloned.1.call-update) | async-done | bytes 262160 | tf_op jit(solution)/shard_map/psum | solution.py:154
  (280 shorter events, 334.8 us)
Async XLA Ops:
  94.9 42.8 %all-to-all-start.1 = ((f32[8,1,49152]{2,1,0:T(1,128)}), f32[8,1,49152]{2,1,0:T(1,128)S(1)}, u32[]{:S(2)}, u32[]{:S(2)}) async-start(f32[8,1,49152]{2,1,0:T(1,128)} %reshape.564), calls=%async_computation.1 | async-start | bytes 3145728 | tf_op jit(solution)/shard_map/all_to_all | solution.py:88
  332.1 20.3 %slice-start = ((s8[6291456]{0:T(1024)(128)(4,1)}), s8[4194304]{0:T(1024)(128)(4,1)S(1)}, s32[]{:S(2)}) async-start(s8[6291456]{0:T(1024)(128)(4,1)} %bitcast.291), calls=%async_computation.6 | async-start | bytes 8388608
  342.1 10.3 %slice-start.1 = ((s8[6291456]{0:T(1024)(128)(4,1)}), s8[2097152]{0:T(1024)(128)(4,1)S(1)}, s32[]{:S(2)}) async-start(s8[6291456]{0:T(1024)(128)(4,1)} %bitcast.291), calls=%async_computation.7 | async-start | bytes 4194304
  396.7 4.9 copy-start.9
  396.7 40.9 %all-to-all-start.3 = ((f32[4,1,196608]{2,1,0:T(1,128)}), f32[4,1,196608]{2,1,0:T(1,128)}, u32[]{:S(2)}, u32[]{:S(2)}) async-start(f32[4,1,196608]{2,1,0:T(1,128)} %reshape.568), calls=%async_computation.3 | async-start | bytes 6291456 | tf_op jit(solution)/shard_map/all_to_all | solution.py:124
  401.5 358.1 %all-reduce.5.cloned.1.call-start = ((), (), s32[]{:S(2)}) async-start(), calls=%async_computation.4 | async-start | bytes 524288 | tf_op jit(solution)/shard_map/psum | solution.py:154
  517.8 4.0 copy-start.5
  521.7 4.4 copy-start.4
  538.4 4.0 copy-start.5
  542.4 4.4 copy-start.4
  559.1 4.0 copy-start.5
  563.1 4.4 copy-start.4
  579.8 4.0 copy-start.5
  583.7 4.3 copy-start.4
  600.4 4.0 copy-start.5
  604.4 4.4 copy-start.4
  621.1 4.0 copy-start.5
  625.1 4.4 copy-start.4
  641.8 4.0 copy-start.5
  645.8 4.4 copy-start.4
  666.4 4.3 copy-start.4
  677.4 41.9 %copy-start.8 = (f32[256,256]{1,0:T(8,128)}, f32[256,256]{1,0:T(8,128)S(1)}, u32[]{:S(2)}) copy-start(f32[256,256]{1,0:T(8,128)S(1)} %get-tuple-element.243) | copy-start | bytes 786436
  719.4 97.6 %all-reduce.7.cloned.1.call-start = ((), (), s32[]{:S(2)}) async-start(), calls=%async_computation.5 | async-start | bytes 524288 | tf_op jit(solution)/shard_map/psum | solution.py:154
  720.0 98.7 %copy-start.1 = (f32[3,1,16,32,128]{4,3,2,1,0:T(8,128)S(1)}, f32[3,1,16,32,128]{4,3,2,1,0:T(8,128)}, u32[]{:S(2)}) copy-start(f32[3,1,16,32,128]{4,3,2,1,0:T(8,128)} %param.10) | copy-start | bytes 2359300
  (39 other events, 110.6 us)
Sparse Core Ops, SparseCore 0:
  719.5 40.1 all-reduce.4
  762.1 54.8 all-reduce.6
